TPU v7x, 32 devices: a whole 2x2x4 slice. The times are simulated.
32 devices in a mesh: kcol: 8 (over y, x, core), ion: 4 (over z).
Axes of the slice: x: 2, y: 2, z: 4, core: 2. Of those that a mesh axis runs over, the one named last changes fastest.
Arguments:
- ions: float32 [4, 81920], P(None, ('kcol', 'ion')), may hold values from -1.5 to 1.5, as said below
- col_ids: int32 [1024], P('kcol'), may hold values from 0 to 4095, as said below
Outputs:
- ion_forces: float32 [4, 81920], P(None, ('kcol', 'ion'))
- energy: float32 [], replicated
Inputs may be any that keep to these rules, and one draw needn't show every extreme that they name: `col_ids`: distinct column numbers. `ions`: rows 0 to 2 lie in [0, 1); row 3 has magnitudes 0.5 to 1.5.
All inputs are finite; a program needn't handle non-finite values.
Results may differ from a plain program's by a relative error of at most 0.0003.
Values sent between devices are 32-bit elements; how exact they have to be, the bound alone decides.
No kernel may reach another device: no remote copies, remote signals or barrier semaphores. Data moves between devices by JAX's collectives and lax.ppermute only.
A program may use at most 64 MiB of HBM per device.

v0:
```python
import math
import jax
import jax.numpy as jnp
from jax import lax
from jax.sharding import PartitionSpec as P

KX = 32


def wave_numbers(col_ids):
    wave_x = jnp.arange(KX, dtype=jnp.int32)
    wave_y = col_ids // 64 - 32
    wave_z = col_ids % 64 - 32
    return (wave_x, wave_y, wave_z)


def kspace_weight(wave_x, wave_y, wave_z):
    radial = wave_y * wave_y + wave_z * wave_z
    along = wave_x * wave_x
    squared = along[:, None] + radial[None, :]
    inside = (squared <= 1024) & (squared > 0)
    squared_f = squared.astype(jnp.float32)
    halving = jnp.where(wave_x == 0, jnp.float32(0.5), jnp.float32(1.0))[:, None]
    return jnp.where(
        inside,
        halving * jnp.exp(-squared_f / 1600.0) / jnp.maximum(squared_f, 1.0),
        jnp.float32(0.0),
    )


def phase_tables(block, wave_x, wave_y, wave_z):
    two_pi = 2.0 * math.pi
    angle_x = two_pi * wave_x.astype(jnp.float32)[:, None] * block[0][None, :]
    angle_yz = two_pi * (
        wave_y.astype(jnp.float32)[:, None] * block[1][None, :]
        + wave_z.astype(jnp.float32)[:, None] * block[2][None, :]
    )
    return (jnp.cos(angle_x), jnp.sin(angle_x), jnp.cos(angle_yz), jnp.sin(angle_yz))


def factor_piece(block, waves):
    cos_x, sin_x, cos_yz, sin_yz = phase_tables(block, *waves)
    charge = block[3][None, :]
    left = jnp.concatenate([charge * cos_x, charge * sin_x], 0)
    right = jnp.concatenate([cos_yz, sin_yz], 0)
    product = lax.dot_general(
        left,
        right,
        (((1,), (1,)), ((), ())),
        precision=lax.Precision.HIGHEST,
        preferred_element_type=jnp.float32,
    )
    nwave = cos_x.shape[0]
    ncol = cos_yz.shape[0]
    real_part = product[:nwave, :ncol] - product[nwave:, ncol:]
    imag_part = product[:nwave, ncol:] + product[nwave:, :ncol]
    return jnp.stack([real_part, imag_part])


def combine_matrix(weight, factor, wave_x):
    g_real = weight * factor[0]
    g_imag = -weight * factor[1]
    scaled = wave_x.astype(jnp.float32)[:, None]
    x_real = scaled * g_real
    x_imag = scaled * g_imag
    return jnp.concatenate(
        [
            jnp.concatenate([g_real.T, -g_imag.T], 1),
            jnp.concatenate([g_imag.T, g_real.T], 1),
            jnp.concatenate([x_real.T, -x_imag.T], 1),
            jnp.concatenate([x_imag.T, x_real.T], 1),
        ],
        0,
    )


def force_piece(block, combined, waves, force_scale, potential_scale):
    cos_x, sin_x, cos_yz, sin_yz = phase_tables(block, *waves)
    basis = jnp.concatenate([cos_x, sin_x], 0)
    spread = jnp.dot(
        combined, basis, precision=lax.Precision.HIGHEST, preferred_element_type=jnp.float32
    )
    ncol = cos_yz.shape[0]
    h_real0 = spread[:ncol]
    h_imag0 = spread[ncol : 2 * ncol]
    h_real1 = spread[2 * ncol : 3 * ncol]
    h_imag1 = spread[3 * ncol :]
    imag_zero = h_real0 * sin_yz + h_imag0 * cos_yz
    real_zero = h_real0 * cos_yz - h_imag0 * sin_yz
    imag_one = h_real1 * sin_yz + h_imag1 * cos_yz
    charge = block[3]
    wave_y = waves[1].astype(jnp.float32)[:, None]
    wave_z = waves[2].astype(jnp.float32)[:, None]
    force_x = force_scale * charge * jnp.sum(imag_one, 0)
    force_y = force_scale * charge * jnp.sum(wave_y * imag_zero, 0)
    force_z = force_scale * charge * jnp.sum(wave_z * imag_zero, 0)
    potential = potential_scale * jnp.sum(real_zero, 0)
    return jnp.stack([force_x, force_y, force_z, potential])


def per_device(ions, col_ids):
    groups = lax.axis_size("kcol")
    piece = ions.shape[1]
    total = piece * groups * lax.axis_size("ion")
    waves = wave_numbers(col_ids)
    weight = kspace_weight(*waves)
    ncol = col_ids.shape[0]
    gathered = lax.all_gather(ions, "kcol", axis=1, tiled=True)

    def add_factor(piece_index, partial_value):
        block = lax.dynamic_slice_in_dim(gathered, piece_index * piece, piece, 1)
        return partial_value + factor_piece(block, waves)

    partial_value = lax.fori_loop(0, groups, add_factor, jnp.zeros((2, KX, ncol), jnp.float32))
    factor = lax.psum(partial_value, "ion")
    energy_group = jnp.float32(0.01 / total) * jnp.sum(
        weight * (factor[0] * factor[0] + factor[1] * factor[1])
    )
    combined = combine_matrix(weight, factor, waves[0])
    force_scale = jnp.float32(0.04 * math.pi / math.sqrt(total))
    potential_scale = jnp.float32(0.4 / math.sqrt(total))

    def place_forces(piece_index, result):
        block = lax.dynamic_slice_in_dim(gathered, piece_index * piece, piece, 1)
        return lax.dynamic_update_slice_in_dim(
            result,
            force_piece(block, combined, waves, force_scale, potential_scale),
            piece_index * piece,
            1,
        )

    row_forces = lax.fori_loop(0, groups, place_forces, jnp.zeros((4, groups * piece), jnp.float32))
    summed, energy = lax.psum((row_forces, energy_group), "kcol")
    owned = lax.dynamic_slice_in_dim(summed, lax.axis_index("kcol") * piece, piece, 1)
    return (owned, energy)


def solution(mesh):
    return jax.shard_map(
        per_device,
        mesh=mesh,
        in_specs=(P(None, ("kcol", "ion")), P("kcol")),
        out_specs=(P(None, ("kcol", "ion")), P()),
        check_vma=False,
    )
```

profile of v0, /device:TPU:0, one launch (start us, length us, event | category | flops | bytes accessed | tf_op | source)
XLA Modules:
  0.0 265.6 jit_solution(9668760638139759695)
XLA Ops:
  7.9 11.2 %all_gather.3 = f32[4,20480]{1,0:T(4,128)S(1)} all-gather(f32[4,2560]{1,0:T(4,128)} %param.6), channel_id=1, replica_groups=mesh['kcol'=8,'ion'=4] {'kcol'}, dimensions={1}, use_global_device_ids=true | all-gather | bytes 368640 | tf_op jit(solution)/shard_map/all_gather | solution.py:108
  19.1 70.5 %while.33 = (s32[]{:T(128)}, f32[2,32,128]{2,1,0:T(8,128)S(1)}, f32[4,20480]{1,0:T(4,128)S(1)}, f32[128,1]{0,1:T(1,128)S(1)}, f32[128,1]{0,1:T(1,128)S(1)}, /*in...) while((s32[]{:T(128)}, f32[2,32,128]{2,1,0:T(8,128)S(1)}, ...), condition=%wide.region_1.2_spmd.clone, body=%wide.region_0.1_spmd.clone.sunk | while | flops 505724992 | bytes 6940129 | solution.py:114
  19.2 4.8 %fusion.62 = (f32[128,2560]{1,0:T(8,128)S(1)}, f32[128,2560]{1,0:T(8,128)S(1)}) fusion(f32[2560]{0:T(1024)S(1)} %get-tuple-element.535, f32[128]{0:T(128)S(1)} %bitcast.69, f32[2560]{0:T(1024)S(1)} %get-tuple-element.536, f32[128]{0:T(128)S(1)} %bitcast.71), kind=kLoop, calls=%fused_computation.37.clone.1 | loop fusion | flops 1310720 | bytes 2642944 | tf_op jit(solution)/shard_map/while/body/eval_jaxpr/cos | solution.py:38
  25.3 2.5 fusion.65
  28.1 4.8 %fusion.62 = (f32[128,2560]{1,0:T(8,128)S(1)}, f32[128,2560]{1,0:T(8,128)S(1)}) fusion(f32[2560]{0:T(1024)S(1)} %get-tuple-element.535, f32[128]{0:T(128)S(1)} %bitcast.69, f32[2560]{0:T(1024)S(1)} %get-tuple-element.536, f32[128]{0:T(128)S(1)} %bitcast.71), kind=kLoop, calls=%fused_computation.37.clone.1 | loop fusion | flops 1310720 | bytes 2642944 | tf_op jit(solution)/shard_map/while/body/eval_jaxpr/cos | solution.py:38
  36.9 4.8 %fusion.62 = (f32[128,2560]{1,0:T(8,128)S(1)}, f32[128,2560]{1,0:T(8,128)S(1)}) fusion(f32[2560]{0:T(1024)S(1)} %get-tuple-element.535, f32[128]{0:T(128)S(1)} %bitcast.69, f32[2560]{0:T(1024)S(1)} %get-tuple-element.536, f32[128]{0:T(128)S(1)} %bitcast.71), kind=kLoop, calls=%fused_computation.37.clone.1 | loop fusion | flops 1310720 | bytes 2642944 | tf_op jit(solution)/shard_map/while/body/eval_jaxpr/cos | solution.py:38
  43.0 2.5 fusion.65
  45.7 4.8 %fusion.62 = (f32[128,2560]{1,0:T(8,128)S(1)}, f32[128,2560]{1,0:T(8,128)S(1)}) fusion(f32[2560]{0:T(1024)S(1)} %get-tuple-element.535, f32[128]{0:T(128)S(1)} %bitcast.69, f32[2560]{0:T(1024)S(1)} %get-tuple-element.536, f32[128]{0:T(128)S(1)} %bitcast.71), kind=kLoop, calls=%fused_computation.37.clone.1 | loop fusion | flops 1310720 | bytes 2642944 | tf_op jit(solution)/shard_map/while/body/eval_jaxpr/cos | solution.py:38
  54.5 4.8 %fusion.62 = (f32[128,2560]{1,0:T(8,128)S(1)}, f32[128,2560]{1,0:T(8,128)S(1)}) fusion(f32[2560]{0:T(1024)S(1)} %get-tuple-element.535, f32[128]{0:T(128)S(1)} %bitcast.69, f32[2560]{0:T(1024)S(1)} %get-tuple-element.536, f32[128]{0:T(128)S(1)} %bitcast.71), kind=kLoop, calls=%fused_computation.37.clone.1 | loop fusion | flops 1310720 | bytes 2642944 | tf_op jit(solution)/shard_map/while/body/eval_jaxpr/cos | solution.py:38
  63.3 4.8 %fusion.62 = (f32[128,2560]{1,0:T(8,128)S(1)}, f32[128,2560]{1,0:T(8,128)S(1)}) fusion(f32[2560]{0:T(1024)S(1)} %get-tuple-element.535, f32[128]{0:T(128)S(1)} %bitcast.69, f32[2560]{0:T(1024)S(1)} %get-tuple-element.536, f32[128]{0:T(128)S(1)} %bitcast.71), kind=kLoop, calls=%fused_computation.37.clone.1 | loop fusion | flops 1310720 | bytes 2642944 | tf_op jit(solution)/shard_map/while/body/eval_jaxpr/cos | solution.py:38
  72.2 4.8 %fusion.62 = (f32[128,2560]{1,0:T(8,128)S(1)}, f32[128,2560]{1,0:T(8,128)S(1)}) fusion(f32[2560]{0:T(1024)S(1)} %get-tuple-element.535, f32[128]{0:T(128)S(1)} %bitcast.69, f32[2560]{0:T(1024)S(1)} %get-tuple-element.536, f32[128]{0:T(128)S(1)} %bitcast.71), kind=kLoop, calls=%fused_computation.37.clone.1 | loop fusion | flops 1310720 | bytes 2642944 | tf_op jit(solution)/shard_map/while/body/eval_jaxpr/cos | solution.py:38
  81.0 4.8 %fusion.62 = (f32[128,2560]{1,0:T(8,128)S(1)}, f32[128,2560]{1,0:T(8,128)S(1)}) fusion(f32[2560]{0:T(1024)S(1)} %get-tuple-element.535, f32[128]{0:T(128)S(1)} %bitcast.69, f32[2560]{0:T(1024)S(1)} %get-tuple-element.536, f32[128]{0:T(128)S(1)} %bitcast.71), kind=kLoop, calls=%fused_computation.37.clone.1 | loop fusion | flops 1310720 | bytes 2642944 | tf_op jit(solution)/shard_map/while/body/eval_jaxpr/cos | solution.py:38
  89.6 19.3 %psum.21 = f32[2,32,128]{2,1,0:T(8,128)S(1)} all-reduce(f32[2,32,128]{2,1,0:T(8,128)S(1)} %get-tuple-element.329), channel_id=1, replica_groups=mesh['kcol'=8,'ion'=4] {'ion'}, use_global_device_ids=true, to_apply=%region_2.3 | all-reduce | flops 8192 | bytes 65536 | tf_op jit(solution)/shard_map/psum | solution.py:115
  109.9 95.1 %while.32 = (s32[]{:T(128)}, f32[4,20480]{1,0:T(4,128)S(1)}, f32[4,20480]{1,0:T(4,128)S(1)}, f32[512,64]{1,0:T(8,128)S(1)}, f32[128,1]{0,1:T(1,128)S(1)}, /*inde...) while((s32[]{:T(128)}, f32[4,20480]{1,0:T(4,128)S(1)}, ...), condition=%wide.region_8.9_spmd.clone, body=%wide.region_3.8_spmd.clone.sunk | while | flops 1013137984 | bytes 12256743 | solution.py:132
  111.2 4.3 %convolution_bitcast_fusion.2 = f32[512,2560]{1,0:T(8,128)S(1)} fusion(f32[512,64]{1,0:T(8,128)S(1)} %get-tuple-element.610, f32[32,2560]{1,0:T(8,128)S(1)} %get-tuple-element.519, f32[32,2560]{1,0:T(8,128)S(1)} %get-tuple-element.520), kind=kOutput, calls=%fused_computation.2.clone.1 | convolution fusion | flops 1006796800 | bytes 6029312 | tf_op jit(solution)/shard_map/while/body/eval_jaxpr/dot_general | solution.py:80
  115.6 6.0 %multiply_reduce_fusion.4 = (f32[2560]{0:T(1024)S(1)}, f32[2560]{0:T(1024)S(1)}, f32[2560]{0:T(1024)S(1)}, f32[2560]{0:T(1024)S(1)}) fusion(f32[128]{0:T(128)S(1)} %bitcast.72, f32[128]{0:T(128)S(1)} %bitcast.70, f32[512,2560]{1,0:T(8,128)S(1)} %convolution_bitcast_fusion.2, f32[2560]{0:T(1024)S(1)} %get-tuple-element.521, f32[2560]{0:T(1024)S(1)} %get-tuple-element.522), kind=kLoop, calls=%fused_computation.9.clone.1 | loop fusion | flops 6215680 | bytes 5305344 | tf_op jit(solution)/shard_map/while/body/eval_jaxpr/reduce_sum | solution.py:95
  123.1 4.3 %convolution_bitcast_fusion.2 = f32[512,2560]{1,0:T(8,128)S(1)} fusion(f32[512,64]{1,0:T(8,128)S(1)} %get-tuple-element.610, f32[32,2560]{1,0:T(8,128)S(1)} %get-tuple-element.519, f32[32,2560]{1,0:T(8,128)S(1)} %get-tuple-element.520), kind=kOutput, calls=%fused_computation.2.clone.1 | convolution fusion | flops 1006796800 | bytes 6029312 | tf_op jit(solution)/shard_map/while/body/eval_jaxpr/dot_general | solution.py:80
  127.5 6.0 %multiply_reduce_fusion.4 = (f32[2560]{0:T(1024)S(1)}, f32[2560]{0:T(1024)S(1)}, f32[2560]{0:T(1024)S(1)}, f32[2560]{0:T(1024)S(1)}) fusion(f32[128]{0:T(128)S(1)} %bitcast.72, f32[128]{0:T(128)S(1)} %bitcast.70, f32[512,2560]{1,0:T(8,128)S(1)} %convolution_bitcast_fusion.2, f32[2560]{0:T(1024)S(1)} %get-tuple-element.521, f32[2560]{0:T(1024)S(1)} %get-tuple-element.522), kind=kLoop, calls=%fused_computation.9.clone.1 | loop fusion | flops 6215680 | bytes 5305344 | tf_op jit(solution)/shard_map/while/body/eval_jaxpr/reduce_sum | solution.py:95
  135.0 4.3 %convolution_bitcast_fusion.2 = f32[512,2560]{1,0:T(8,128)S(1)} fusion(f32[512,64]{1,0:T(8,128)S(1)} %get-tuple-element.610, f32[32,2560]{1,0:T(8,128)S(1)} %get-tuple-element.519, f32[32,2560]{1,0:T(8,128)S(1)} %get-tuple-element.520), kind=kOutput, calls=%fused_computation.2.clone.1 | convolution fusion | flops 1006796800 | bytes 6029312 | tf_op jit(solution)/shard_map/while/body/eval_jaxpr/dot_general | solution.py:80
  139.4 6.0 %multiply_reduce_fusion.4 = (f32[2560]{0:T(1024)S(1)}, f32[2560]{0:T(1024)S(1)}, f32[2560]{0:T(1024)S(1)}, f32[2560]{0:T(1024)S(1)}) fusion(f32[128]{0:T(128)S(1)} %bitcast.72, f32[128]{0:T(128)S(1)} %bitcast.70, f32[512,2560]{1,0:T(8,128)S(1)} %convolution_bitcast_fusion.2, f32[2560]{0:T(1024)S(1)} %get-tuple-element.521, f32[2560]{0:T(1024)S(1)} %get-tuple-element.522), kind=kLoop, calls=%fused_computation.9.clone.1 | loop fusion | flops 6215680 | bytes 5305344 | tf_op jit(solution)/shard_map/while/body/eval_jaxpr/reduce_sum | solution.py:95
  146.9 4.3 %convolution_bitcast_fusion.2 = f32[512,2560]{1,0:T(8,128)S(1)} fusion(f32[512,64]{1,0:T(8,128)S(1)} %get-tuple-element.610, f32[32,2560]{1,0:T(8,128)S(1)} %get-tuple-element.519, f32[32,2560]{1,0:T(8,128)S(1)} %get-tuple-element.520), kind=kOutput, calls=%fused_computation.2.clone.1 | convolution fusion | flops 1006796800 | bytes 6029312 | tf_op jit(solution)/shard_map/while/body/eval_jaxpr/dot_general | solution.py:80
  151.2 6.0 %multiply_reduce_fusion.4 = (f32[2560]{0:T(1024)S(1)}, f32[2560]{0:T(1024)S(1)}, f32[2560]{0:T(1024)S(1)}, f32[2560]{0:T(1024)S(1)}) fusion(f32[128]{0:T(128)S(1)} %bitcast.72, f32[128]{0:T(128)S(1)} %bitcast.70, f32[512,2560]{1,0:T(8,128)S(1)} %convolution_bitcast_fusion.2, f32[2560]{0:T(1024)S(1)} %get-tuple-element.521, f32[2560]{0:T(1024)S(1)} %get-tuple-element.522), kind=kLoop, calls=%fused_computation.9.clone.1 | loop fusion | flops 6215680 | bytes 5305344 | tf_op jit(solution)/shard_map/while/body/eval_jaxpr/reduce_sum | solution.py:95
  158.8 4.3 %convolution_bitcast_fusion.2 = f32[512,2560]{1,0:T(8,128)S(1)} fusion(f32[512,64]{1,0:T(8,128)S(1)} %get-tuple-element.610, f32[32,2560]{1,0:T(8,128)S(1)} %get-tuple-element.519, f32[32,2560]{1,0:T(8,128)S(1)} %get-tuple-element.520), kind=kOutput, calls=%fused_computation.2.clone.1 | convolution fusion | flops 1006796800 | bytes 6029312 | tf_op jit(solution)/shard_map/while/body/eval_jaxpr/dot_general | solution.py:80
  163.1 6.0 %multiply_reduce_fusion.4 = (f32[2560]{0:T(1024)S(1)}, f32[2560]{0:T(1024)S(1)}, f32[2560]{0:T(1024)S(1)}, f32[2560]{0:T(1024)S(1)}) fusion(f32[128]{0:T(128)S(1)} %bitcast.72, f32[128]{0:T(128)S(1)} %bitcast.70, f32[512,2560]{1,0:T(8,128)S(1)} %convolution_bitcast_fusion.2, f32[2560]{0:T(1024)S(1)} %get-tuple-element.521, f32[2560]{0:T(1024)S(1)} %get-tuple-element.522), kind=kLoop, calls=%fused_computation.9.clone.1 | loop fusion | flops 6215680 | bytes 5305344 | tf_op jit(solution)/shard_map/while/body/eval_jaxpr/reduce_sum | solution.py:95
  170.7 4.3 %convolution_bitcast_fusion.2 = f32[512,2560]{1,0:T(8,128)S(1)} fusion(f32[512,64]{1,0:T(8,128)S(1)} %get-tuple-element.610, f32[32,2560]{1,0:T(8,128)S(1)} %get-tuple-element.519, f32[32,2560]{1,0:T(8,128)S(1)} %get-tuple-element.520), kind=kOutput, calls=%fused_computation.2.clone.1 | convolution fusion | flops 1006796800 | bytes 6029312 | tf_op jit(solution)/shard_map/while/body/eval_jaxpr/dot_general | solution.py:80
  175.0 6.0 %multiply_reduce_fusion.4 = (f32[2560]{0:T(1024)S(1)}, f32[2560]{0:T(1024)S(1)}, f32[2560]{0:T(1024)S(1)}, f32[2560]{0:T(1024)S(1)}) fusion(f32[128]{0:T(128)S(1)} %bitcast.72, f32[128]{0:T(128)S(1)} %bitcast.70, f32[512,2560]{1,0:T(8,128)S(1)} %convolution_bitcast_fusion.2, f32[2560]{0:T(1024)S(1)} %get-tuple-element.521, f32[2560]{0:T(1024)S(1)} %get-tuple-element.522), kind=kLoop, calls=%fused_computation.9.clone.1 | loop fusion | flops 6215680 | bytes 5305344 | tf_op jit(solution)/shard_map/while/body/eval_jaxpr/reduce_sum | solution.py:95
  182.6 4.3 %convolution_bitcast_fusion.2 = f32[512,2560]{1,0:T(8,128)S(1)} fusion(f32[512,64]{1,0:T(8,128)S(1)} %get-tuple-element.610, f32[32,2560]{1,0:T(8,128)S(1)} %get-tuple-element.519, f32[32,2560]{1,0:T(8,128)S(1)} %get-tuple-element.520), kind=kOutput, calls=%fused_computation.2.clone.1 | convolution fusion | flops 1006796800 | bytes 6029312 | tf_op jit(solution)/shard_map/while/body/eval_jaxpr/dot_general | solution.py:80
  186.9 6.0 %multiply_reduce_fusion.4 = (f32[2560]{0:T(1024)S(1)}, f32[2560]{0:T(1024)S(1)}, f32[2560]{0:T(1024)S(1)}, f32[2560]{0:T(1024)S(1)}) fusion(f32[128]{0:T(128)S(1)} %bitcast.72, f32[128]{0:T(128)S(1)} %bitcast.70, f32[512,2560]{1,0:T(8,128)S(1)} %convolution_bitcast_fusion.2, f32[2560]{0:T(1024)S(1)} %get-tuple-element.521, f32[2560]{0:T(1024)S(1)} %get-tuple-element.522), kind=kLoop, calls=%fused_computation.9.clone.1 | loop fusion | flops 6215680 | bytes 5305344 | tf_op jit(solution)/shard_map/while/body/eval_jaxpr/reduce_sum | solution.py:95
  194.5 4.3 %convolution_bitcast_fusion.2 = f32[512,2560]{1,0:T(8,128)S(1)} fusion(f32[512,64]{1,0:T(8,128)S(1)} %get-tuple-element.610, f32[32,2560]{1,0:T(8,128)S(1)} %get-tuple-element.519, f32[32,2560]{1,0:T(8,128)S(1)} %get-tuple-element.520), kind=kOutput, calls=%fused_computation.2.clone.1 | convolution fusion | flops 1006796800 | bytes 6029312 | tf_op jit(solution)/shard_map/while/body/eval_jaxpr/dot_general | solution.py:80
  198.8 6.0 %multiply_reduce_fusion.4 = (f32[2560]{0:T(1024)S(1)}, f32[2560]{0:T(1024)S(1)}, f32[2560]{0:T(1024)S(1)}, f32[2560]{0:T(1024)S(1)}) fusion(f32[128]{0:T(128)S(1)} %bitcast.72, f32[128]{0:T(128)S(1)} %bitcast.70, f32[512,2560]{1,0:T(8,128)S(1)} %convolution_bitcast_fusion.2, f32[2560]{0:T(1024)S(1)} %get-tuple-element.521, f32[2560]{0:T(1024)S(1)} %get-tuple-element.522), kind=kLoop, calls=%fused_computation.9.clone.1 | loop fusion | flops 6215680 | bytes 5305344 | tf_op jit(solution)/shard_map/while/body/eval_jaxpr/reduce_sum | solution.py:95
  206.4 12.4 %psum.23 = f32[]{:T(128)} all-reduce(f32[]{:T(128)S(6)} %mul_shard_map.3), channel_id=1, replica_groups=mesh['kcol'=8,'ion'=4] {'kcol'}, use_global_device_ids=true, to_apply=%region_11.12 | all-reduce | flops 1 | bytes 8 | tf_op jit(solution)/shard_map/psum | solution.py:133
  218.8 38.5 %all-reduce.2.cloned.1.call-done = f32[4,20480]{1,0:T(4,128)} async-done(((f32[4,20480]{1,0:T(4,128)}), f32[4,20480]{1,0:T(4,128)}) %all-reduce.2.cloned.1.call-update) | async-done | bytes 327696 | tf_op jit(solution)/shard_map/psum | solution.py:133
  (117 shorter events, 42.4 us)
Async XLA Ops:
  7.2 250.2 %all-reduce.2.cloned.1.call-start = ((), (), s32[]{:S(2)}) async-start(), calls=%async_computation | async-start | bytes 655360 | tf_op jit(solution)/shard_map/psum | solution.py:133
  205.0 0.7 copy-start
Sparse Core Ops, SparseCore 0:
  205.9 51.3 all-reduce.1
where the time goes:
time: 266 us
  other arithmetic  109 us (41%)
  matrix products  54.6 us (21%)
  blocking collectives  42.8 us (16%)
  waiting for transfers between devices  38.5 us (14%)
  between operations  14.8 us (6%)
  local copies, waits for them, and re-layouts  4.71 us (2%)
    reduce_sum x8, other arithmetic, force_piece(): force_y = force_scale * charge * jnp.sum(wave_y * imag_zero, 0)  47.9 us
    cos x8, other arithmetic, phase_tables(): jnp.cos(angle_yz)  38.6 us
    psum x1, waiting for transfers between devices, per_device(): summed, energy = lax.psum((row_forces, energy_group), 'kcol')  38.5 us
    dot_general x8, matrix products, force_piece(): jnp.dot(combined, basis, precision=lax.Precision.HIGHEST, preferred_eleme...  34.5 us
    dot_general x8, matrix products, factor_piece(): lax.dot_general(left, right, (((1,), (1,)), ((), ())), precision=lax.Prec...  20.1 us
    psum x1, blocking collectives, per_device(): factor = lax.psum(partial_value, 'ion')  19.3 us
    psum x1, blocking collectives, per_device(): summed, energy = lax.psum((row_forces, energy_group), 'kcol')  12.4 us
    all_gather x1, blocking collectives, per_device(): gathered = lax.all_gather(ions, 'kcol', axis=1, tiled=True)  11.2 us
  transfers between devices with their start and end apart: 1, of which 1 were waited for; matrix products, arithmetic and copies ran while one was open for 0% of the time, Pallas kernels for 0%

commit v1 on v0

--- a/solution.py
+++ b/solution.py
@@ -5,6 +5,11 @@
 from jax.sharding import PartitionSpec as P
 
 KX = 32
+
+
+def add_all(value, axis):
+    parts = lax.all_gather(value, axis)
+    return jnp.sum(parts, axis=0)
 
 
 def wave_numbers(col_ids):
@@ -112,7 +117,7 @@
         return partial_value + factor_piece(block, waves)
 
     partial_value = lax.fori_loop(0, groups, add_factor, jnp.zeros((2, KX, ncol), jnp.float32))
-    factor = lax.psum(partial_value, "ion")
+    factor = add_all(partial_value, "ion")
     energy_group = jnp.float32(0.01 / total) * jnp.sum(
         weight * (factor[0] * factor[0] + factor[1] * factor[1])
     )

time: 266 us -> 263 us (0.989)
  blocking collectives: 42.8 us -> 37.3 us
  waiting for transfers between devices: 38.5 us -> 41.5 us
    psum x1 -> x0, blocking collectives: 19.3 us -> none  [per_device(): factor = lax.psum(partial_value, 'ion')]
    all_gather x0 -> x1, blocking collectives: none -> 13.8 us  [add_all(): parts = lax.all_gather(value, axis)]
    psum x1, waiting for transfers between devices: 38.5 us -> 41.5 us  [per_device(): summed, energy = lax.psum((row_forces, energy_group), 'kcol')]
where the time goes in v1:
time: 263 us
  other arithmetic  109 us (41%)
  matrix products  54.6 us (21%)
  waiting for transfers between devices  41.5 us (16%)
  blocking collectives  37.3 us (14%)
  between operations  14.7 us (6%)
  local copies, waits for them, and re-layouts  4.71 us (2%)
    reduce_sum x8, other arithmetic, force_piece(): force_y = force_scale * charge * jnp.sum(wave_y * imag_zero, 0)  47.9 us
    psum x1, waiting for transfers between devices, per_device(): summed, energy = lax.psum((row_forces, energy_group), 'kcol')  41.5 us
    cos x8, other arithmetic, phase_tables(): jnp.cos(angle_yz)  38.6 us
    dot_general x8, matrix products, force_piece(): jnp.dot(combined, basis, precision=lax.Precision.HIGHEST, preferred_eleme...  34.5 us
    dot_general x8, matrix products, factor_piece(): lax.dot_general(left, right, (((1,), (1,)), ((), ())), precision=lax.Prec...  20.1 us
    all_gather x1, blocking collectives, add_all(): parts = lax.all_gather(value, axis)  13.8 us
    psum x1, blocking collectives, per_device(): summed, energy = lax.psum((row_forces, energy_group), 'kcol')  12.3 us
    all_gather x1, blocking collectives, per_device(): gathered = lax.all_gather(ions, 'kcol', axis=1, tiled=True)  11.2 us
  transfers between devices with their start and end apart: 1, of which 1 were waited for; matrix products, arithmetic and copies ran while one was open for 0% of the time, Pallas kernels for 0%

profile of v1, /device:TPU:0, one launch (start us, length us, event | category | flops | bytes accessed | tf_op | source)
XLA Modules:
  0.0 263.0 jit_solution(4078933226962645434)
XLA Ops:
  7.9 11.2 %all_gather.9 = f32[4,20480]{1,0:T(4,128)S(1)} all-gather(f32[4,2560]{1,0:T(4,128)} %param.6), channel_id=1, replica_groups=mesh['kcol'=8,'ion'=4] {'kcol'}, dimensions={1}, use_global_device_ids=true | all-gather | bytes 368640 | tf_op jit(solution)/shard_map/all_gather | solution.py:113
  19.1 70.5 %while.33 = (s32[]{:T(128)}, f32[2,32,128]{2,1,0:T(8,128)S(1)}, f32[4,20480]{1,0:T(4,128)S(1)}, f32[128,1]{0,1:T(1,128)S(1)}, f32[128,1]{0,1:T(1,128)S(1)}, /*in...) while((s32[]{:T(128)}, f32[2,32,128]{2,1,0:T(8,128)S(1)}, ...), condition=%wide.region_1.2_spmd.clone, body=%wide.region_0.1_spmd.clone.sunk | while | flops 505724992 | bytes 6940129 | solution.py:119
  19.2 4.8 %fusion.62 = (f32[128,2560]{1,0:T(8,128)S(1)}, f32[128,2560]{1,0:T(8,128)S(1)}) fusion(f32[2560]{0:T(1024)S(1)} %get-tuple-element.535, f32[128]{0:T(128)S(1)} %bitcast.71, f32[2560]{0:T(1024)S(1)} %get-tuple-element.536, f32[128]{0:T(128)S(1)} %bitcast.73), kind=kLoop, calls=%fused_computation.37.clone.1 | loop fusion | flops 1310720 | bytes 2642944 | tf_op jit(solution)/shard_map/while/body/eval_jaxpr/cos | solution.py:43
  25.3 2.5 fusion.65
  28.1 4.8 %fusion.62 = (f32[128,2560]{1,0:T(8,128)S(1)}, f32[128,2560]{1,0:T(8,128)S(1)}) fusion(f32[2560]{0:T(1024)S(1)} %get-tuple-element.535, f32[128]{0:T(128)S(1)} %bitcast.71, f32[2560]{0:T(1024)S(1)} %get-tuple-element.536, f32[128]{0:T(128)S(1)} %bitcast.73), kind=kLoop, calls=%fused_computation.37.clone.1 | loop fusion | flops 1310720 | bytes 2642944 | tf_op jit(solution)/shard_map/while/body/eval_jaxpr/cos | solution.py:43
  36.9 4.8 %fusion.62 = (f32[128,2560]{1,0:T(8,128)S(1)}, f32[128,2560]{1,0:T(8,128)S(1)}) fusion(f32[2560]{0:T(1024)S(1)} %get-tuple-element.535, f32[128]{0:T(128)S(1)} %bitcast.71, f32[2560]{0:T(1024)S(1)} %get-tuple-element.536, f32[128]{0:T(128)S(1)} %bitcast.73), kind=kLoop, calls=%fused_computation.37.clone.1 | loop fusion | flops 1310720 | bytes 2642944 | tf_op jit(solution)/shard_map/while/body/eval_jaxpr/cos | solution.py:43
  43.0 2.5 fusion.65
  45.7 4.8 %fusion.62 = (f32[128,2560]{1,0:T(8,128)S(1)}, f32[128,2560]{1,0:T(8,128)S(1)}) fusion(f32[2560]{0:T(1024)S(1)} %get-tuple-element.535, f32[128]{0:T(128)S(1)} %bitcast.71, f32[2560]{0:T(1024)S(1)} %get-tuple-element.536, f32[128]{0:T(128)S(1)} %bitcast.73), kind=kLoop, calls=%fused_computation.37.clone.1 | loop fusion | flops 1310720 | bytes 2642944 | tf_op jit(solution)/shard_map/while/body/eval_jaxpr/cos | solution.py:43
  54.5 4.8 %fusion.62 = (f32[128,2560]{1,0:T(8,128)S(1)}, f32[128,2560]{1,0:T(8,128)S(1)}) fusion(f32[2560]{0:T(1024)S(1)} %get-tuple-element.535, f32[128]{0:T(128)S(1)} %bitcast.71, f32[2560]{0:T(1024)S(1)} %get-tuple-element.536, f32[128]{0:T(128)S(1)} %bitcast.73), kind=kLoop, calls=%fused_computation.37.clone.1 | loop fusion | flops 1310720 | bytes 2642944 | tf_op jit(solution)/shard_map/while/body/eval_jaxpr/cos | solution.py:43
  63.3 4.8 %fusion.62 = (f32[128,2560]{1,0:T(8,128)S(1)}, f32[128,2560]{1,0:T(8,128)S(1)}) fusion(f32[2560]{0:T(1024)S(1)} %get-tuple-element.535, f32[128]{0:T(128)S(1)} %bitcast.71, f32[2560]{0:T(1024)S(1)} %get-tuple-element.536, f32[128]{0:T(128)S(1)} %bitcast.73), kind=kLoop, calls=%fused_computation.37.clone.1 | loop fusion | flops 1310720 | bytes 2642944 | tf_op jit(solution)/shard_map/while/body/eval_jaxpr/cos | solution.py:43
  72.2 4.8 %fusion.62 = (f32[128,2560]{1,0:T(8,128)S(1)}, f32[128,2560]{1,0:T(8,128)S(1)}) fusion(f32[2560]{0:T(1024)S(1)} %get-tuple-element.535, f32[128]{0:T(128)S(1)} %bitcast.71, f32[2560]{0:T(1024)S(1)} %get-tuple-element.536, f32[128]{0:T(128)S(1)} %bitcast.73), kind=kLoop, calls=%fused_computation.37.clone.1 | loop fusion | flops 1310720 | bytes 2642944 | tf_op jit(solution)/shard_map/while/body/eval_jaxpr/cos | solution.py:43
  81.0 4.8 %fusion.62 = (f32[128,2560]{1,0:T(8,128)S(1)}, f32[128,2560]{1,0:T(8,128)S(1)}) fusion(f32[2560]{0:T(1024)S(1)} %get-tuple-element.535, f32[128]{0:T(128)S(1)} %bitcast.71, f32[2560]{0:T(1024)S(1)} %get-tuple-element.536, f32[128]{0:T(128)S(1)} %bitcast.73), kind=kLoop, calls=%fused_computation.37.clone.1 | loop fusion | flops 1310720 | bytes 2642944 | tf_op jit(solution)/shard_map/while/body/eval_jaxpr/cos | solution.py:43
  89.6 13.8 %all-gather = f32[8,32,128]{2,1,0:T(8,128)S(1)} all-gather(f32[2,32,128]{2,1,0:T(8,128)S(1)} %get-tuple-element.329), channel_id=2, replica_groups=mesh['kcol'=8,'ion'=4] {'ion'}, dimensions={0}, use_global_device_ids=true | all-gather | bytes 163840 | tf_op jit(solution)/shard_map/all_gather | solution.py:11
  104.4 95.1 %while.32 = (s32[]{:T(128)}, f32[4,20480]{1,0:T(4,128)S(1)}, f32[4,20480]{1,0:T(4,128)S(1)}, f32[512,64]{1,0:T(8,128)S(1)}, f32[128,1]{0,1:T(1,128)S(1)}, /*inde...) while((s32[]{:T(128)}, f32[4,20480]{1,0:T(4,128)S(1)}, ...), condition=%wide.region_8.9_spmd.clone, body=%wide.region_3.8_spmd.clone.sunk | while | flops 1013137984 | bytes 12256743 | solution.py:137
  105.8 4.3 %convolution_bitcast_fusion.2 = f32[512,2560]{1,0:T(8,128)S(1)} fusion(f32[512,64]{1,0:T(8,128)S(1)} %get-tuple-element.610, f32[32,2560]{1,0:T(8,128)S(1)} %get-tuple-element.519, f32[32,2560]{1,0:T(8,128)S(1)} %get-tuple-element.520), kind=kOutput, calls=%fused_computation.2.clone.1 | convolution fusion | flops 1006796800 | bytes 6029312 | tf_op jit(solution)/shard_map/while/body/eval_jaxpr/dot_general | solution.py:85
  110.1 6.0 %multiply_reduce_fusion.4 = (f32[2560]{0:T(1024)S(1)}, f32[2560]{0:T(1024)S(1)}, f32[2560]{0:T(1024)S(1)}, f32[2560]{0:T(1024)S(1)}) fusion(f32[128]{0:T(128)S(1)} %bitcast.74, f32[128]{0:T(128)S(1)} %bitcast.72, f32[512,2560]{1,0:T(8,128)S(1)} %convolution_bitcast_fusion.2, f32[2560]{0:T(1024)S(1)} %get-tuple-element.521, f32[2560]{0:T(1024)S(1)} %get-tuple-element.522), kind=kLoop, calls=%fused_computation.9.clone.1 | loop fusion | flops 6215680 | bytes 5305344 | tf_op jit(solution)/shard_map/while/body/eval_jaxpr/reduce_sum | solution.py:100
  117.7 4.3 %convolution_bitcast_fusion.2 = f32[512,2560]{1,0:T(8,128)S(1)} fusion(f32[512,64]{1,0:T(8,128)S(1)} %get-tuple-element.610, f32[32,2560]{1,0:T(8,128)S(1)} %get-tuple-element.519, f32[32,2560]{1,0:T(8,128)S(1)} %get-tuple-element.520), kind=kOutput, calls=%fused_computation.2.clone.1 | convolution fusion | flops 1006796800 | bytes 6029312 | tf_op jit(solution)/shard_map/while/body/eval_jaxpr/dot_general | solution.py:85
  122.0 6.0 %multiply_reduce_fusion.4 = (f32[2560]{0:T(1024)S(1)}, f32[2560]{0:T(1024)S(1)}, f32[2560]{0:T(1024)S(1)}, f32[2560]{0:T(1024)S(1)}) fusion(f32[128]{0:T(128)S(1)} %bitcast.74, f32[128]{0:T(128)S(1)} %bitcast.72, f32[512,2560]{1,0:T(8,128)S(1)} %convolution_bitcast_fusion.2, f32[2560]{0:T(1024)S(1)} %get-tuple-element.521, f32[2560]{0:T(1024)S(1)} %get-tuple-element.522), kind=kLoop, calls=%fused_computation.9.clone.1 | loop fusion | flops 6215680 | bytes 5305344 | tf_op jit(solution)/shard_map/while/body/eval_jaxpr/reduce_sum | solution.py:100
  129.5 4.3 %convolution_bitcast_fusion.2 = f32[512,2560]{1,0:T(8,128)S(1)} fusion(f32[512,64]{1,0:T(8,128)S(1)} %get-tuple-element.610, f32[32,2560]{1,0:T(8,128)S(1)} %get-tuple-element.519, f32[32,2560]{1,0:T(8,128)S(1)} %get-tuple-element.520), kind=kOutput, calls=%fused_computation.2.clone.1 | convolution fusion | flops 1006796800 | bytes 6029312 | tf_op jit(solution)/shard_map/while/body/eval_jaxpr/dot_general | solution.py:85
  133.9 6.0 %multiply_reduce_fusion.4 = (f32[2560]{0:T(1024)S(1)}, f32[2560]{0:T(1024)S(1)}, f32[2560]{0:T(1024)S(1)}, f32[2560]{0:T(1024)S(1)}) fusion(f32[128]{0:T(128)S(1)} %bitcast.74, f32[128]{0:T(128)S(1)} %bitcast.72, f32[512,2560]{1,0:T(8,128)S(1)} %convolution_bitcast_fusion.2, f32[2560]{0:T(1024)S(1)} %get-tuple-element.521, f32[2560]{0:T(1024)S(1)} %get-tuple-element.522), kind=kLoop, calls=%fused_computation.9.clone.1 | loop fusion | flops 6215680 | bytes 5305344 | tf_op jit(solution)/shard_map/while/body/eval_jaxpr/reduce_sum | solution.py:100
  141.4 4.3 %convolution_bitcast_fusion.2 = f32[512,2560]{1,0:T(8,128)S(1)} fusion(f32[512,64]{1,0:T(8,128)S(1)} %get-tuple-element.610, f32[32,2560]{1,0:T(8,128)S(1)} %get-tuple-element.519, f32[32,2560]{1,0:T(8,128)S(1)} %get-tuple-element.520), kind=kOutput, calls=%fused_computation.2.clone.1 | convolution fusion | flops 1006796800 | bytes 6029312 | tf_op jit(solution)/shard_map/while/body/eval_jaxpr/dot_general | solution.py:85
  145.8 6.0 %multiply_reduce_fusion.4 = (f32[2560]{0:T(1024)S(1)}, f32[2560]{0:T(1024)S(1)}, f32[2560]{0:T(1024)S(1)}, f32[2560]{0:T(1024)S(1)}) fusion(f32[128]{0:T(128)S(1)} %bitcast.74, f32[128]{0:T(128)S(1)} %bitcast.72, f32[512,2560]{1,0:T(8,128)S(1)} %convolution_bitcast_fusion.2, f32[2560]{0:T(1024)S(1)} %get-tuple-element.521, f32[2560]{0:T(1024)S(1)} %get-tuple-element.522), kind=kLoop, calls=%fused_computation.9.clone.1 | loop fusion | flops 6215680 | bytes 5305344 | tf_op jit(solution)/shard_map/while/body/eval_jaxpr/reduce_sum | solution.py:100
  153.3 4.3 %convolution_bitcast_fusion.2 = f32[512,2560]{1,0:T(8,128)S(1)} fusion(f32[512,64]{1,0:T(8,128)S(1)} %get-tuple-element.610, f32[32,2560]{1,0:T(8,128)S(1)} %get-tuple-element.519, f32[32,2560]{1,0:T(8,128)S(1)} %get-tuple-element.520), kind=kOutput, calls=%fused_computation.2.clone.1 | convolution fusion | flops 1006796800 | bytes 6029312 | tf_op jit(solution)/shard_map/while/body/eval_jaxpr/dot_general | solution.py:85
  157.7 6.0 %multiply_reduce_fusion.4 = (f32[2560]{0:T(1024)S(1)}, f32[2560]{0:T(1024)S(1)}, f32[2560]{0:T(1024)S(1)}, f32[2560]{0:T(1024)S(1)}) fusion(f32[128]{0:T(128)S(1)} %bitcast.74, f32[128]{0:T(128)S(1)} %bitcast.72, f32[512,2560]{1,0:T(8,128)S(1)} %convolution_bitcast_fusion.2, f32[2560]{0:T(1024)S(1)} %get-tuple-element.521, f32[2560]{0:T(1024)S(1)} %get-tuple-element.522), kind=kLoop, calls=%fused_computation.9.clone.1 | loop fusion | flops 6215680 | bytes 5305344 | tf_op jit(solution)/shard_map/while/body/eval_jaxpr/reduce_sum | solution.py:100
  165.2 4.3 %convolution_bitcast_fusion.2 = f32[512,2560]{1,0:T(8,128)S(1)} fusion(f32[512,64]{1,0:T(8,128)S(1)} %get-tuple-element.610, f32[32,2560]{1,0:T(8,128)S(1)} %get-tuple-element.519, f32[32,2560]{1,0:T(8,128)S(1)} %get-tuple-element.520), kind=kOutput, calls=%fused_computation.2.clone.1 | convolution fusion | flops 1006796800 | bytes 6029312 | tf_op jit(solution)/shard_map/while/body/eval_jaxpr/dot_general | solution.py:85
  169.5 6.0 %multiply_reduce_fusion.4 = (f32[2560]{0:T(1024)S(1)}, f32[2560]{0:T(1024)S(1)}, f32[2560]{0:T(1024)S(1)}, f32[2560]{0:T(1024)S(1)}) fusion(f32[128]{0:T(128)S(1)} %bitcast.74, f32[128]{0:T(128)S(1)} %bitcast.72, f32[512,2560]{1,0:T(8,128)S(1)} %convolution_bitcast_fusion.2, f32[2560]{0:T(1024)S(1)} %get-tuple-element.521, f32[2560]{0:T(1024)S(1)} %get-tuple-element.522), kind=kLoop, calls=%fused_computation.9.clone.1 | loop fusion | flops 6215680 | bytes 5305344 | tf_op jit(solution)/shard_map/while/body/eval_jaxpr/reduce_sum | solution.py:100
  177.1 4.3 %convolution_bitcast_fusion.2 = f32[512,2560]{1,0:T(8,128)S(1)} fusion(f32[512,64]{1,0:T(8,128)S(1)} %get-tuple-element.610, f32[32,2560]{1,0:T(8,128)S(1)} %get-tuple-element.519, f32[32,2560]{1,0:T(8,128)S(1)} %get-tuple-element.520), kind=kOutput, calls=%fused_computation.2.clone.1 | convolution fusion | flops 1006796800 | bytes 6029312 | tf_op jit(solution)/shard_map/while/body/eval_jaxpr/dot_general | solution.py:85
  181.4 6.0 %multiply_reduce_fusion.4 = (f32[2560]{0:T(1024)S(1)}, f32[2560]{0:T(1024)S(1)}, f32[2560]{0:T(1024)S(1)}, f32[2560]{0:T(1024)S(1)}) fusion(f32[128]{0:T(128)S(1)} %bitcast.74, f32[128]{0:T(128)S(1)} %bitcast.72, f32[512,2560]{1,0:T(8,128)S(1)} %convolution_bitcast_fusion.2, f32[2560]{0:T(1024)S(1)} %get-tuple-element.521, f32[2560]{0:T(1024)S(1)} %get-tuple-element.522), kind=kLoop, calls=%fused_computation.9.clone.1 | loop fusion | flops 6215680 | bytes 5305344 | tf_op jit(solution)/shard_map/while/body/eval_jaxpr/reduce_sum | solution.py:100
  189.0 4.3 %convolution_bitcast_fusion.2 = f32[512,2560]{1,0:T(8,128)S(1)} fusion(f32[512,64]{1,0:T(8,128)S(1)} %get-tuple-element.610, f32[32,2560]{1,0:T(8,128)S(1)} %get-tuple-element.519, f32[32,2560]{1,0:T(8,128)S(1)} %get-tuple-element.520), kind=kOutput, calls=%fused_computation.2.clone.1 | convolution fusion | flops 1006796800 | bytes 6029312 | tf_op jit(solution)/shard_map/while/body/eval_jaxpr/dot_general | solution.py:85
  193.3 6.0 %multiply_reduce_fusion.4 = (f32[2560]{0:T(1024)S(1)}, f32[2560]{0:T(1024)S(1)}, f32[2560]{0:T(1024)S(1)}, f32[2560]{0:T(1024)S(1)}) fusion(f32[128]{0:T(128)S(1)} %bitcast.74, f32[128]{0:T(128)S(1)} %bitcast.72, f32[512,2560]{1,0:T(8,128)S(1)} %convolution_bitcast_fusion.2, f32[2560]{0:T(1024)S(1)} %get-tuple-element.521, f32[2560]{0:T(1024)S(1)} %get-tuple-element.522), kind=kLoop, calls=%fused_computation.9.clone.1 | loop fusion | flops 6215680 | bytes 5305344 | tf_op jit(solution)/shard_map/while/body/eval_jaxpr/reduce_sum | solution.py:100
  200.9 12.3 %psum.15 = f32[]{:T(128)} all-reduce(f32[]{:T(128)S(6)} %mul_shard_map.3), channel_id=1, replica_groups=mesh['kcol'=8,'ion'=4] {'kcol'}, use_global_device_ids=true, to_apply=%region_11.12 | all-reduce | flops 1 | bytes 8 | tf_op jit(solution)/shard_map/psum | solution.py:138
  213.3 41.5 %all-reduce.2.cloned.1.call-done = f32[4,20480]{1,0:T(4,128)} async-done(((f32[4,20480]{1,0:T(4,128)}), f32[4,20480]{1,0:T(4,128)}) %all-reduce.2.cloned.1.call-update) | async-done | bytes 327696 | tf_op jit(solution)/shard_map/psum | solution.py:138
  (118 shorter events, 42.4 us)
Async XLA Ops:
  7.2 247.6 %all-reduce.2.cloned.1.call-start = ((), (), s32[]{:S(2)}) async-start(), calls=%async_computation | async-start | bytes 655360 | tf_op jit(solution)/shard_map/psum | solution.py:138
  199.5 0.7 copy-start
Sparse Core Ops, SparseCore 0:
  200.4 54.2 all-reduce.1
